TPU v7x, 128 devices: a whole 4x4x4 slice. The times are simulated.
128 devices in a mesh: req: 64 (over y, z, x), tp: 2 (over core).
Axes of the slice: x: 4, y: 4, z: 4, core: 2. Of those that a mesh axis runs over, the one named last changes fastest.
Arguments:
- tokens: bfloat16 [12288, 1536], P('req', 'tp'), may hold values from -6 to 6
- video_lengths: int32 [5], replicated, may hold values from 1 to 7680, 12288 in all
- timestep: int32 [1], replicated, may hold values from 1 to 1000
- time_weight: float32 [256, 4608], replicated, may hold values from -0.375 to 0.375
- block_mod: float32 [3, 1536], replicated, may hold values from -3 to 3
- w_query: bfloat16 [1536, 1536], P(None, 'tp')
- w_key: bfloat16 [1536, 1536], P(None, 'tp')
- w_value: bfloat16 [1536, 1536], P(None, 'tp'), may hold values from -0.15625 to 0.15625
- w_out: bfloat16 [1536, 1536], P('tp'), may hold values from -0.15625 to 0.15625
Outputs:
- velocity: bfloat16 [12288, 1536], P('req', 'tp')
- stepped: bfloat16 [12288, 1536], P('req', 'tp')
Inputs may be any that keep to these rules, and one draw needn't show every extreme that they name: `video_lengths`: the videos' lengths in packing order; they sum to 12288 and the longest has exactly 7680 tokens.
All inputs are finite; a program needn't handle non-finite values.
Results may differ from a plain program's by a relative error of at most 0.017.
Values may be sent and summed in bfloat16 or wider, within the bound.
A program may use at most 256 MiB of HBM per device.

v0:
```python
import math
import jax
import jax.numpy as jnp
from jax import lax
from jax.sharding import PartitionSpec as P

HEAD_DIM = 128
STEPS = 1000


def noise_level(step_value):
    frac = step_value / STEPS
    return 5.0 * frac / (1.0 + 4.0 * frac)


def on_device(
    tokens, video_lengths, timestep, time_weight, block_mod, w_query, w_key, w_value, w_out
):
    tok_rows = tokens.shape[0]
    width = time_weight.shape[1] // 3
    full_rows = lax.all_gather(tokens, "tp", axis=1, tiled=True)
    time_value = timestep[0].astype(jnp.float32)
    sigma = noise_level(time_value)
    delta_sigma = noise_level(time_value - 1.0) - sigma
    half_freq = time_weight.shape[0] // 2
    frequency = jnp.exp(-math.log(10000.0) * jnp.arange(half_freq, dtype=jnp.float32) / half_freq)
    angle = 1000.0 * sigma * frequency
    embedding = jnp.concatenate([jnp.cos(angle), jnp.sin(angle)])
    modulation = jnp.dot(
        jax.nn.silu(embedding)[None, :],
        time_weight,
        precision=lax.Precision.HIGHEST,
        preferred_element_type=jnp.float32,
    )[0]
    modulation = modulation.reshape(3, width) + block_mod
    shift, scale, gate = (modulation[0], modulation[1], modulation[2])
    as_float = full_rows.astype(jnp.float32)
    mean = jnp.mean(as_float, axis=1, keepdims=True)
    centred = as_float - mean
    variance = jnp.mean(centred * centred, axis=1, keepdims=True)
    normed = (centred * lax.rsqrt(variance + 1e-06) * (1.0 + scale) + shift).astype(jnp.bfloat16)
    query = jnp.dot(normed, w_query, preferred_element_type=jnp.float32).astype(jnp.bfloat16)
    keys = jnp.dot(normed, w_key, preferred_element_type=jnp.float32).astype(jnp.bfloat16)
    values = jnp.dot(normed, w_value, preferred_element_type=jnp.float32).astype(jnp.bfloat16)
    heads_here = query.shape[1] // HEAD_DIM
    query_heads = query.reshape(tok_rows, heads_here, HEAD_DIM)
    start_row = lax.axis_index("req") * tok_rows
    query_index = start_row + jnp.arange(tok_rows, dtype=jnp.int32)
    video_ends = jnp.cumsum(video_lengths)
    video_starts = video_ends - video_lengths
    inside = jnp.logical_and(
        query_index[:, None] >= video_starts[None, :], query_index[:, None] < video_ends[None, :]
    )
    query_low = jnp.sum(jnp.where(inside, video_starts[None, :], 0), axis=1)
    query_high = jnp.sum(jnp.where(inside, video_ends[None, :], 0), axis=1)
    key_index = jnp.arange(tok_rows * lax.psum(1, "req"), dtype=jnp.int32)
    valid = jnp.logical_and(
        key_index[None, :] >= query_low[:, None], key_index[None, :] < query_high[:, None]
    )
    outputs = []
    for head in range(heads_here):
        cols = slice(head * HEAD_DIM, (head + 1) * HEAD_DIM)
        packed = jnp.concatenate([keys[:, cols], values[:, cols]], axis=1)
        gathered = lax.all_gather(packed, "req", axis=0, tiled=True)
        key_head = gathered[:, :HEAD_DIM]
        value_head = gathered[:, HEAD_DIM:]
        scores = jnp.dot(
            query[:, cols], key_head.T, preferred_element_type=jnp.float32
        ) / math.sqrt(HEAD_DIM)
        row_max = jnp.max(jnp.where(valid, scores, -1e30), axis=1, keepdims=True)
        probs = jnp.where(valid, jnp.exp(scores - row_max), 0.0)
        row_sum = jnp.sum(probs, axis=1, keepdims=True)
        weighted = jnp.dot(
            probs.astype(jnp.bfloat16), value_head, preferred_element_type=jnp.float32
        )
        outputs.append((weighted / row_sum).astype(jnp.bfloat16))
    attended = jnp.concatenate(outputs, axis=1)
    partial_value = jnp.dot(attended, w_out, preferred_element_type=jnp.float32)
    own_sum = lax.psum_scatter(
        partial_value.astype(jnp.bfloat16), "tp", scatter_dimension=1, tiled=True
    ).astype(jnp.float32)
    share = own_sum.shape[1]
    gate_share = lax.dynamic_slice_in_dim(gate, lax.axis_index("tp") * share, share)
    branch = gate_share[None, :] * own_sum
    velocity = branch.astype(jnp.bfloat16)
    stepped = (tokens.astype(jnp.float32) + delta_sigma * branch).astype(jnp.bfloat16)
    return (velocity, stepped)


def solution(mesh):
    return jax.shard_map(
        on_device,
        mesh=mesh,
        in_specs=(
            P("req", "tp"),
            P(),
            P(),
            P(),
            P(),
            P(None, "tp"),
            P(None, "tp"),
            P(None, "tp"),
            P("tp", None),
        ),
        out_specs=(P("req", "tp"), P("req", "tp")),
        check_vma=False,
    )
```

profile of v0, /device:TPU:1, one launch (start us, length us, event | category | flops | bytes accessed | tf_op | source)
XLA Modules:
  0.0 568.4 jit_solution(9086971898280065333)
XLA Ops:
  8.1 3.5 all_gather.21
  12.1 6.0 %copy.12 = f32[256,4608]{0,1:T(8,128)} copy(f32[256,4608]{1,0:T(8,128)} %param.12) | data formatting | bytes 9437184 | tf_op args[3]
  18.2 6.4 %fusion.172 = f32[1,3,1536]{2,0,1:T(1,128)S(1)} fusion(f32[256,1,1]{0,1,2:T(1,128)S(1)} %bitcast.27, f32[3,1536,256]{2,1,0:T(8,128)} %bitcast.24), kind=kOutput, calls=%fused_computation.133 | convolution fusion | flops 14155776 | bytes 4738048 | tf_op jit(solution)/shard_map/dot_general | solution.py:29
  24.6 2.4 convolution_convert_fusion.2
  35.1 67.6 %all-gather.7.cloned.1.call-done = bf16[12288,256]{1,0:T(8,128)(2,1)} async-done(((bf16[192,256]{1,0:T(8,128)(2,1)}), bf16[12288,256]{1,0:T(8,128)(2,1)}) %all-gather.7.cloned.1.call-update) | async-done | bytes 6291472 | tf_op jit(solution)/shard_map/all_gather | solution.py:64
  102.7 6.9 %convolution_multiply_fusion.5 = f32[192,12288]{1,0:T(8,128)} fusion(bf16[12288,256]{1,0:T(8,128)(2,1)} %all-gather.7.cloned.1.call-done, bf16[192,768]{1,0:T(8,128)(2,1)S(1)} %convolution_convert_fusion.3), kind=kOutput, calls=%fused_computation.5 | convolution fusion | flops 606339072 | bytes 12632064 | tf_op jit(solution)/shard_map/dot_general | solution.py:67
  109.7 67.4 %all-gather.11.cloned.1.call-done = bf16[12288,256]{1,0:T(8,128)(2,1)} async-done(((bf16[192,256]{1,0:T(8,128)(2,1)}), bf16[12288,256]{1,0:T(8,128)(2,1)}) %all-gather.11.cloned.1.call-update) | async-done | bytes 6291472 | tf_op jit(solution)/shard_map/all_gather | solution.py:64
  177.0 6.9 %convolution_multiply_fusion.3 = f32[192,12288]{1,0:T(8,128)} fusion(bf16[12288,256]{1,0:T(8,128)(2,1)} %all-gather.11.cloned.1.call-done, bf16[192,768]{1,0:T(8,128)(2,1)S(1)} %convolution_convert_fusion.3), kind=kOutput, calls=%fused_computation.3 | convolution fusion | flops 606339072 | bytes 12632064 | tf_op jit(solution)/shard_map/dot_general | solution.py:67
  184.0 67.4 %all-gather.13.cloned.1.call-done = bf16[12288,256]{1,0:T(8,128)(2,1)} async-done(((bf16[192,256]{1,0:T(8,128)(2,1)}), bf16[12288,256]{1,0:T(8,128)(2,1)}) %all-gather.13.cloned.1.call-update) | async-done | bytes 6291472 | tf_op jit(solution)/shard_map/all_gather | solution.py:64
  251.3 7.0 %convolution_multiply_fusion.2 = f32[192,12288]{1,0:T(8,128)} fusion(bf16[12288,256]{1,0:T(8,128)(2,1)} %all-gather.13.cloned.1.call-done, bf16[192,768]{1,0:T(8,128)(2,1)S(1)} %convolution_convert_fusion.3), kind=kOutput, calls=%fused_computation.2 | convolution fusion | flops 606339072 | bytes 12632064 | tf_op jit(solution)/shard_map/dot_general | solution.py:67
  258.3 67.1 %all-gather.15.cloned.1.call-done = bf16[12288,256]{1,0:T(8,128)(2,1)} async-done(((bf16[192,256]{1,0:T(8,128)(2,1)}), bf16[12288,256]{1,0:T(8,128)(2,1)}) %all-gather.15.cloned.1.call-update) | async-done | bytes 6291472 | tf_op jit(solution)/shard_map/all_gather | solution.py:64
  325.5 6.8 %convolution_multiply_fusion.1 = f32[192,12288]{1,0:T(8,128)} fusion(bf16[12288,256]{1,0:T(8,128)(2,1)} %all-gather.15.cloned.1.call-done, bf16[192,768]{1,0:T(8,128)(2,1)S(1)} %convolution_convert_fusion.3), kind=kOutput, calls=%fused_computation.1 | convolution fusion | flops 606339072 | bytes 12632064 | tf_op jit(solution)/shard_map/dot_general | solution.py:67
  332.3 67.9 %all-gather.17.cloned.1.call-done = bf16[12288,256]{1,0:T(8,128)(2,1)} async-done(((bf16[192,256]{1,0:T(8,128)(2,1)}), bf16[12288,256]{1,0:T(8,128)(2,1)}) %all-gather.17.cloned.1.call-update) | async-done | bytes 6291472 | tf_op jit(solution)/shard_map/all_gather | solution.py:64
  400.2 13.5 %select_reduce_fusion = (f32[192]{0:T(256)S(1)}, f32[192]{0:T(256)S(1)}, f32[192,12288]{1,0:T(8,128)}) fusion(s32[192]{0:T(256)S(1)} %get-tuple-element.17, s32[192]{0:T(256)S(1)} %get-tuple-element.16, f32[192,12288]{1,0:T(8,128)} %convolution_multiply_fusion.5, bf16[12288,256]{1,0:T(8,128)(2,1)} %all-gather.17.cloned.1.call-done, ...), kind=kOutput, calls=%fused_computation.7 | convolution fusion | flops 622853760 | bytes 22072832 | tf_op jit(solution)/shard_map/dot_general | solution.py:67
  413.6 60.7 %all-gather.9.cloned.1.call-done = bf16[12288,256]{1,0:T(8,128)(2,1)} async-done(((bf16[192,256]{1,0:T(8,128)(2,1)}), bf16[12288,256]{1,0:T(8,128)(2,1)}) %all-gather.9.cloned.1.call-update) | async-done | bytes 6291472 | tf_op jit(solution)/shard_map/all_gather | solution.py:64
  474.3 23.0 %fusion.11 = (f32[192]{0:T(256)S(1)}, f32[192]{0:T(256)S(1)}, f32[192]{0:T(256)S(1)}, f32[192]{0:T(256)S(1)}, f32[192]{0:T(256)S(1)}, /*index=5*/f32[192]{0:T(256)S(1)}, f32[192,12288]{1,0:T(8,128)}) fusion(f32[192,12288]{1,0:T(8,128)} %get-tuple-element.33, f32[192]{0:T(256)S(1)} %get-tuple-element.10, s32[192]{0:T(256)S(1)} %get-tuple-element.17, ...), kind=kOutput, calls=%fused_computation.31 | convolution fusion | flops 646445952 | bytes 59826688 | tf_op jit(solution)/shard_map/dot_general | solution.py:67
  497.4 13.4 %fusion.9 = (f32[192]{0:T(256)S(1)}, f32[192]{0:T(256)S(1)}, f32[192]{0:T(256)S(1)}, f32[192]{0:T(256)S(1)}) fusion(f32[192,12288]{1,0:T(8,128)S(1)} %bitcast.19, f32[192]{0:T(256)S(1)} %get-tuple-element.8, s32[192]{0:T(256)S(1)} %get-tuple-element.17, s32[192]{0:T(256)S(1)} %get-tuple-element.16, f32[192,12288]{1,0:T(8,128)} %get-tuple-element.34, ...), kind=kLoop, calls=%fused_computation.29 | loop fusion | flops 35388672 | bytes 37756416 | tf_op jit(solution)/shard_map/reduce_sum | solution.py:72
  510.9 7.7 %fusion.65 = bf16[192,768]{1,0:T(8,128)(2,1)S(1)} fusion(bf16[12288,256]{1,0:T(8,128)(2,1)} %all-gather.7.cloned.1.call-done, f32[192,12288]{1,0:T(8,128)} %convolution_multiply_fusion.5, f32[192]{0:T(256)S(1)} %get-tuple-element.11, f32[192]{0:T(256)S(1)} %get-tuple-element.9, s32[192]{0:T(256)S(1)} %get-tuple-element.17, s32[192]{0:T(256)S(1)} %get-tuple-element.16), kind=kOutput, calls=%fused_computation.77 | convolution fusion | flops 618184704 | bytes 12635136 | tf_op jit(solution)/shard_map/dot_general | solution.py:73
  518.6 7.8 %fusion.80 = bf16[192,768]{1,0:T(8,128)(2,1)S(1)} fusion(bf16[192,768]{1,0:T(8,128)(2,1)S(1)} %fusion.65, bf16[12288,256]{1,0:T(8,128)(2,1)} %all-gather.9.cloned.1.call-done, f32[192,12288]{1,0:T(8,128)} %get-tuple-element.34, f32[192]{0:T(256)S(1)} %get-tuple-element.5, f32[192]{0:T(256)S(1)} %get-tuple-element.13, s32[192]{0:T(256)S(1)} %get-tuple-element.17, ...), kind=kOutput, calls=%fused_computation.80 | convolution fusion | flops 618184704 | bytes 12636160 | tf_op jit(solution)/shard_map/dot_general | solution.py:73
  526.4 5.2 fusion.95
  531.7 5.4 fusion.110
  537.1 3.1 fusion.125
  540.3 6.8 %fusion.140 = bf16[192,768]{1,0:T(8,128)(2,1)S(1)} fusion(bf16[192,768]{1,0:T(8,128)(2,1)S(1)} %fusion.125, bf16[12288,256]{1,0:T(8,128)(2,1)S(1)} %bitcast.30, f32[192,12288]{1,0:T(8,128)} %get-tuple-element.33, f32[192]{0:T(256)S(1)} %get-tuple-element.10, f32[192]{0:T(256)S(1)} %get-tuple-element.4, s32[192]{0:T(256)S(1)} %get-tuple-element.17, ...), kind=kOutput, calls=%fused_computation.92 | convolution fusion | flops 618184704 | bytes 12636160 | tf_op jit(solution)/shard_map/dot_general | solution.py:73
  548.7 10.8 %reduce-scatter.2.cloned.1.call-done = bf16[192,768]{1,0:T(8,128)(2,1)} async-done(((bf16[192,1536]{1,0:T(8,128)(2,1)}), bf16[192,768]{1,0:T(8,128)(2,1)}) %reduce-scatter.2.cloned.1.call-update) | async-done | bytes 294928 | tf_op jit(solution)/shard_map/reduce_scatter | solution.py:79
  (80 shorter events, 12.1 us)
Async XLA Ops:
  7.2 540.0 %copy-start = (bf16[768,1536]{1,0:T(8,128)(2,1)S(1)}, bf16[768,1536]{1,0:T(8,128)(2,1)}, u32[]{:S(2)}) copy-start(bf16[768,1536]{1,0:T(8,128)(2,1)} %param.17) | copy-start | bytes 7077892
  7.2 95.6 %all-gather.7.cloned.1.call-start = ((), (), s32[]{:S(2)}) async-start(), calls=%async_computation.1 | async-start | bytes 6389760 | tf_op jit(solution)/shard_map/all_gather | solution.py:64
  12.1 12.4 %copy-start.2 = (f32[3,1536]{1,0:T(4,128)S(1)}, f32[3,1536]{1,0:T(4,128)}, u32[]{:S(2)}) copy-start(f32[3,1536]{1,0:T(4,128)} %param.13) | copy-start | bytes 55300
  18.1 8.9 %copy-start.3 = (bf16[1536,768]{1,0:T(8,128)(2,1)S(1)}, bf16[1536,768]{1,0:T(8,128)(2,1)}, u32[]{:S(2)}) copy-start(bf16[1536,768]{1,0:T(8,128)(2,1)} %param.16) | copy-start | bytes 7077892
  24.5 7.9 %copy-start.4 = (s32[5]{0:T(128)S(1)}, s32[5]{0:T(128)}, u32[]{:S(2)}) copy-start(s32[5]{0:T(128)} %param.10) | copy-start | bytes 64
  28.6 148.5 %all-gather.11.cloned.1.call-start = ((), (), s32[]{:S(2)}) async-start(), calls=%async_computation.3 | async-start | bytes 6389760 | tf_op jit(solution)/shard_map/all_gather | solution.py:64
  29.3 222.0 %all-gather.13.cloned.1.call-start = ((), (), s32[]{:S(2)}) async-start(), calls=%async_computation.4 | async-start | bytes 6389760 | tf_op jit(solution)/shard_map/all_gather | solution.py:64
  30.1 295.4 %all-gather.15.cloned.1.call-start = ((), (), s32[]{:S(2)}) async-start(), calls=%async_computation.5 | async-start | bytes 6389760 | tf_op jit(solution)/shard_map/all_gather | solution.py:64
  30.8 369.4 %all-gather.17.cloned.1.call-start = ((), (), s32[]{:S(2)}) async-start(), calls=%async_computation.6 | async-start | bytes 6389760 | tf_op jit(solution)/shard_map/all_gather | solution.py:64
  31.5 442.8 %all-gather.9.cloned.1.call-start = ((), (), s32[]{:S(2)}) async-start(), calls=%async_computation.2 | async-start | bytes 6389760 | tf_op jit(solution)/shard_map/all_gather | solution.py:64
  32.2 527.3 %reduce-scatter.2.cloned.1.call-start = ((), (), s32[]{:S(2)}) async-start(), calls=%async_computation.7 | async-start | bytes 884736 | tf_op jit(solution)/shard_map/reduce_scatter | solution.py:79
  474.3 23.0 %slice-start = ((s8[9437184]{0:T(1024)(128)(4,1)}), s8[4194304]{0:T(1024)(128)(4,1)S(1)}, s32[]{:S(2)}) async-start(s8[9437184]{0:T(1024)(128)(4,1)} %bitcast.18), calls=%async_computation.8 | async-start | bytes 8388608
  474.3 23.0 %slice-start.1 = ((s8[9437184]{0:T(1024)(128)(4,1)}), s8[4194304]{0:T(1024)(128)(4,1)S(1)}, s32[]{:S(2)}) async-start(s8[9437184]{0:T(1024)(128)(4,1)} %bitcast.18), calls=%async_computation.9 | async-start | bytes 8388608
  474.3 23.0 %slice-start.2 = ((s8[9437184]{0:T(1024)(128)(4,1)}), s8[1048576]{0:T(1024)(128)(4,1)S(1)}, s32[]{:S(2)}) async-start(s8[9437184]{0:T(1024)(128)(4,1)} %bitcast.18), calls=%async_computation.10 | async-start | bytes 2097152
  510.8 15.6 %slice-start.6 = ((s8[9437184]{0:T(1024)(128)(4,1)}), s8[4194304]{0:T(1024)(128)(4,1)S(1)}, s32[]{:S(2)}) async-start(s8[9437184]{0:T(1024)(128)(4,1)} %bitcast.22), calls=%async_computation.14 | async-start | bytes 8388608
  510.8 15.6 %slice-start.7 = ((s8[9437184]{0:T(1024)(128)(4,1)}), s8[4194304]{0:T(1024)(128)(4,1)S(1)}, s32[]{:S(2)}) async-start(s8[9437184]{0:T(1024)(128)(4,1)} %bitcast.22), calls=%async_computation.15 | async-start | bytes 8388608
  518.6 7.8 %slice-start.8 = ((s8[9437184]{0:T(1024)(128)(4,1)}), s8[1048576]{0:T(1024)(128)(4,1)S(1)}, s32[]{:S(2)}) async-start(s8[9437184]{0:T(1024)(128)(4,1)} %bitcast.22), calls=%async_computation.16 | async-start | bytes 2097152
  518.6 13.1 %slice-start.3 = ((s8[9437184]{0:T(1024)(128)(4,1)}), s8[4194304]{0:T(1024)(128)(4,1)S(1)}, s32[]{:S(2)}) async-start(s8[9437184]{0:T(1024)(128)(4,1)} %bitcast.20), calls=%async_computation.11 | async-start | bytes 8388608
  518.6 13.1 %slice-start.4 = ((s8[9437184]{0:T(1024)(128)(4,1)}), s8[4194304]{0:T(1024)(128)(4,1)S(1)}, s32[]{:S(2)}) async-start(s8[9437184]{0:T(1024)(128)(4,1)} %bitcast.20), calls=%async_computation.12 | async-start | bytes 8388608
  526.4 5.3 slice-start.5
  526.4 10.7 %slice-start.9 = ((s8[6291456]{0:T(1024)(128)(4,1)}), s8[2097152]{0:T(1024)(128)(4,1)S(1)}, s32[]{:S(2)}) async-start(s8[6291456]{0:T(1024)(128)(4,1)} %bitcast.25), calls=%async_computation.17 | async-start | bytes 4194304
  531.7 5.4 slice-start.10
  531.7 8.5 %slice-start.11 = ((s8[6291456]{0:T(1024)(128)(4,1)}), s8[2097152]{0:T(1024)(128)(4,1)S(1)}, s32[]{:S(2)}) async-start(s8[6291456]{0:T(1024)(128)(4,1)} %bitcast.29), calls=%async_computation.19 | async-start | bytes 4194304
  540.3 19.2 %copy-start.1 = (bf16[192,768]{1,0:T(8,128)(2,1)S(1)}, bf16[192,768]{1,0:T(8,128)(2,1)}, u32[]{:S(2)}) copy-start(bf16[192,768]{1,0:T(8,128)(2,1)} %param.9) | copy-start | bytes 884740
  (1 other events, 3.1 us)
Sparse Core Ops, SparseCore 0:
  28.7 74.0 all-gather.6
  105.6 71.4 all-gather.10
  179.9 71.4 all-gather.12
  254.0 71.4 all-gather.14
  328.7 71.4 all-gather.16
  402.9 71.4 all-gather.8
  548.7 10.7 reduce-scatter.1
where the time goes:
time: 574 us; the launch traced here: 568 us
  waiting for transfers between devices  409 us (71%)
  matrix products  114 us (20%)
  other arithmetic  20.1 us (4%)
  between operations  15.6 us (3%)
  local copies, waits for them, and re-layouts  6.26 us (1%)
    all_gather x6, waiting for transfers between devices, on_device(): gathered = lax.all_gather(packed, 'req', axis=0, tiled=True)  398 us
    dot_general x6, matrix products, on_device(): jnp.dot(query[:, cols], key_head.T, preferred_element_type=jnp.float32)  64.1 us
    dot_general x6, matrix products, on_device(): jnp.dot(probs.astype(jnp.bfloat16), value_head, preferred_element_type=jn...  36 us
    reduce_sum x1, other arithmetic, on_device(): row_sum = jnp.sum(probs, axis=1, keepdims=True)  13.4 us
  transfers between devices with their start and end apart: 7, of which 7 were waited for; matrix products, arithmetic and copies ran while one was open for 8% of the time, Pallas kernels for 0%

commit v1 on v0

--- a/solution.py
+++ b/solution.py
@@ -3,6 +3,7 @@
 import jax.numpy as jnp
 from jax import lax
 from jax.sharding import PartitionSpec as P
+from jax.lax import all_to_all, axis_size
 
 HEAD_DIM = 128
 STEPS = 1000
@@ -61,7 +62,10 @@
     for head in range(heads_here):
         cols = slice(head * HEAD_DIM, (head + 1) * HEAD_DIM)
         packed = jnp.concatenate([keys[:, cols], values[:, cols]], axis=1)
-        gathered = lax.all_gather(packed, "req", axis=0, tiled=True)
+        odd = axis_size("req")
+        z_new = jnp.stack(odd * [packed])
+        placed = all_to_all(z_new, "req", split_axis=0, concat_axis=0)
+        gathered = jnp.concatenate(placed, 0)
         key_head = gathered[:, :HEAD_DIM]
         value_head = gathered[:, HEAD_DIM:]
         scores = jnp.dot(

time: 574 us -> 685 us (1.19)
  starting transfers between devices: 0.47 us -> 70.3 us
  local copies, waits for them, and re-layouts: 6.26 us -> 32.3 us
  waiting for transfers between devices: 409 us -> 428 us
    all_to_all x0 -> x6, waiting for transfers between devices: none -> 409 us  [on_device(): placed = all_to_all(z_new, 'req', split_axis=0, concat_axis=0)]
    all_gather x6 -> x0, waiting for transfers between devices: 398 us -> none  [on_device(): gathered = lax.all_gather(packed, 'req', axis=0, tiled=True)]
    all_to_all x0 -> x6, starting transfers between devices: none -> 70.3 us  [on_device(): placed = all_to_all(z_new, 'req', split_axis=0, concat_axis=0)]
    another operation x0 -> x6, local copies, waits for them, and re-layouts: none -> 20.4 us  [on_device(): z_new = jnp.stack(odd * [packed])]
    reduce_scatter x1, waiting for transfers between devices: 10.8 us -> 19.1 us  [on_device(): lax.psum_scatter(partial_value.astype(jnp.bfloat16), 'tp', scatter_dimens...]
  transfers between devices with their start and end apart: 7 -> 7, of which waited for: 7 -> 7; matrix products, arithmetic and copies ran while one was open for 8% -> 6% of each run, Pallas kernels for 0% -> 0%
where the time goes in v1:
time: 685 us; the launch traced here: 676 us
  waiting for transfers between devices  428 us (62%)
  matrix products  111 us (16%)
  starting transfers between devices  70.3 us (10%)
  local copies, waits for them, and re-layouts  32.3 us (5%)
  between operations  15.5 us (2%)
  other arithmetic  15 us (2%)
    all_to_all x6, waiting for transfers between devices, on_device(): placed = all_to_all(z_new, 'req', split_axis=0, concat_axis=0)  409 us
    all_to_all x6, starting transfers between devices, on_device(): placed = all_to_all(z_new, 'req', split_axis=0, concat_axis=0)  70.3 us
    dot_general x6, matrix products, on_device(): jnp.dot(query[:, cols], key_head.T, preferred_element_type=jnp.float32)  57.4 us
    dot_general x6, matrix products, on_device(): jnp.dot(probs.astype(jnp.bfloat16), value_head, preferred_element_type=jn...  40.7 us
    another operation x6, local copies, waits for them, and re-layouts, on_device(): z_new = jnp.stack(odd * [packed])  20.4 us
    reduce_scatter x1, waiting for transfers between devices, on_device(): lax.psum_scatter(partial_value.astype(jnp.bfloat16), 'tp', scatter_dimens...  19.1 us
  transfers between devices with their start and end apart: 7, of which 7 were waited for; matrix products, arithmetic and copies ran while one was open for 6% of the time, Pallas kernels for 0%

profile of v1, /device:TPU:1, one launch (start us, length us, event | category | flops | bytes accessed | tf_op | source)
XLA Modules:
  0.0 675.9 jit_solution(10893559086863316624)
XLA Ops:
  18.1 6.4 fusion.172
  31.3 11.4 %all-to-all-start = ((bf16[64,192,256]{2,1,0:T(8,128)(2,1)}), bf16[64,192,256]{2,1,0:T(8,128)(2,1)}, u32[]{:S(2)}, u32[]{:S(2)}) async-start(bf16[64,192,256]{2,1,0:T(8,128)(2,1)} %stack.12), calls=%async_computation | async-start | bytes 12582912 | tf_op jit(solution)/shard_map/all_to_all | solution.py:67
  42.8 79.3 %all-to-all-done = bf16[64,192,256]{2,1,0:T(8,128)(2,1)} async-done(((bf16[64,192,256]{2,1,0:T(8,128)(2,1)}), bf16[64,192,256]{2,1,0:T(8,128)(2,1)}, u32[]{:S(2)}, u32[]{:S(2)}) %all-to-all-start) | async-done | bytes 6291488 | tf_op jit(solution)/shard_map/all_to_all | solution.py:67
  125.4 8.3 %all-to-all-start.2 = ((bf16[64,192,256]{2,1,0:T(8,128)(2,1)}), bf16[64,192,256]{2,1,0:T(8,128)(2,1)}, u32[]{:S(2)}, u32[]{:S(2)}) async-start(bf16[64,192,256]{2,1,0:T(8,128)(2,1)} %stack.14), calls=%async_computation.2 | async-start | bytes 12582912 | tf_op jit(solution)/shard_map/all_to_all | solution.py:67
  133.8 79.9 %all-to-all-done.2 = bf16[64,192,256]{2,1,0:T(8,128)(2,1)} async-done(((bf16[64,192,256]{2,1,0:T(8,128)(2,1)}), bf16[64,192,256]{2,1,0:T(8,128)(2,1)}, u32[]{:S(2)}, u32[]{:S(2)}) %all-to-all-start.2) | async-done | bytes 6291488 | tf_op jit(solution)/shard_map/all_to_all | solution.py:67
  217.1 10.6 %all-to-all-start.3 = ((bf16[64,192,256]{2,1,0:T(8,128)(2,1)}), bf16[64,192,256]{2,1,0:T(8,128)(2,1)}, u32[]{:S(2)}, u32[]{:S(2)}) async-start(bf16[64,192,256]{2,1,0:T(8,128)(2,1)} %stack.15), calls=%async_computation.3 | async-start | bytes 12582912 | tf_op jit(solution)/shard_map/all_to_all | solution.py:67
  227.7 73.3 %all-to-all-done.3 = bf16[64,192,256]{2,1,0:T(8,128)(2,1)} async-done(((bf16[64,192,256]{2,1,0:T(8,128)(2,1)}), bf16[64,192,256]{2,1,0:T(8,128)(2,1)}, u32[]{:S(2)}, u32[]{:S(2)}) %all-to-all-start.3) | async-done | bytes 6291488 | tf_op jit(solution)/shard_map/all_to_all | solution.py:67
  304.4 12.8 %all-to-all-start.5 = ((bf16[64,192,256]{2,1,0:T(8,128)(2,1)}), bf16[64,192,256]{2,1,0:T(8,128)(2,1)}, u32[]{:S(2)}, u32[]{:S(2)}) async-start(bf16[64,192,256]{2,1,0:T(8,128)(2,1)} %stack.17), calls=%async_computation.5 | async-start | bytes 12582912 | tf_op jit(solution)/shard_map/all_to_all | solution.py:67
  317.2 73.5 %all-to-all-done.5 = bf16[64,192,256]{2,1,0:T(8,128)(2,1)} async-done(((bf16[64,192,256]{2,1,0:T(8,128)(2,1)}), bf16[64,192,256]{2,1,0:T(8,128)(2,1)}, u32[]{:S(2)}, u32[]{:S(2)}) %all-to-all-start.5) | async-done | bytes 6291488 | tf_op jit(solution)/shard_map/all_to_all | solution.py:67
  394.1 13.6 %all-to-all-start.4 = ((bf16[64,192,256]{2,1,0:T(8,128)(2,1)}), bf16[64,192,256]{2,1,0:T(8,128)(2,1)}, u32[]{:S(2)}, u32[]{:S(2)}) async-start(bf16[64,192,256]{2,1,0:T(8,128)(2,1)} %stack.16), calls=%async_computation.4 | async-start | bytes 12582912 | tf_op jit(solution)/shard_map/all_to_all | solution.py:67
  407.7 72.1 %all-to-all-done.4 = bf16[64,192,256]{2,1,0:T(8,128)(2,1)} async-done(((bf16[64,192,256]{2,1,0:T(8,128)(2,1)}), bf16[64,192,256]{2,1,0:T(8,128)(2,1)}, u32[]{:S(2)}, u32[]{:S(2)}) %all-to-all-start.4) | async-done | bytes 6291488 | tf_op jit(solution)/shard_map/all_to_all | solution.py:67
  483.3 13.5 %all-to-all-start.1 = ((bf16[64,192,256]{2,1,0:T(8,128)(2,1)}), bf16[64,192,256]{2,1,0:T(8,128)(2,1)}, u32[]{:S(2)}, u32[]{:S(2)}) async-start(bf16[64,192,256]{2,1,0:T(8,128)(2,1)} %stack.13), calls=%async_computation.1 | async-start | bytes 12582912 | tf_op jit(solution)/shard_map/all_to_all | solution.py:67
  499.5 6.9 %convolution_multiply_fusion.1 = f32[192,12288]{1,0:T(8,128)} fusion(bf16[12288,256]{1,0:T(8,128)(2,1)} %bitcast.11, bf16[192,768]{1,0:T(8,128)(2,1)S(1)} %convolution_convert_fusion.3), kind=kOutput, calls=%fused_computation.1 | convolution fusion | flops 606339072 | bytes 12632064 | tf_op jit(solution)/shard_map/dot_general | solution.py:71
  506.4 7.0 %convolution_multiply_fusion.2 = f32[192,12288]{1,0:T(8,128)} fusion(bf16[12288,256]{1,0:T(8,128)(2,1)} %bitcast.10, bf16[192,768]{1,0:T(8,128)(2,1)S(1)} %convolution_convert_fusion.3), kind=kOutput, calls=%fused_computation.2 | convolution fusion | flops 606339072 | bytes 12632064 | tf_op jit(solution)/shard_map/dot_general | solution.py:71
  513.5 6.9 %convolution_multiply_fusion.3 = f32[192,12288]{1,0:T(8,128)} fusion(bf16[12288,256]{1,0:T(8,128)(2,1)} %bitcast.9, bf16[192,768]{1,0:T(8,128)(2,1)S(1)} %convolution_convert_fusion.3), kind=kOutput, calls=%fused_computation.3 | convolution fusion | flops 606339072 | bytes 12632064 | tf_op jit(solution)/shard_map/dot_general | solution.py:71
  527.2 10.8 %select_reduce_fusion = (f32[192]{0:T(256)S(1)}, f32[192]{0:T(256)S(1)}, f32[192,12288]{1,0:T(8,128)}) fusion(s32[192]{0:T(256)S(1)} %get-tuple-element.17, s32[192]{0:T(256)S(1)} %get-tuple-element.16, f32[192,12288]{1,0:T(8,128)S(1)} %convolution_multiply_fusion.5, bf16[12288,256]{1,0:T(8,128)(2,1)} %bitcast.12, ...), kind=kOutput, calls=%fused_computation.7 | convolution fusion | flops 622853760 | bytes 22072832 | tf_op jit(solution)/shard_map/dot_general | solution.py:71
  537.9 30.9 %all-to-all-done.1 = bf16[64,192,256]{2,1,0:T(8,128)(2,1)} async-done(((bf16[64,192,256]{2,1,0:T(8,128)(2,1)}), bf16[64,192,256]{2,1,0:T(8,128)(2,1)}, u32[]{:S(2)}, u32[]{:S(2)}) %all-to-all-start.1) | async-done | bytes 6291488 | tf_op jit(solution)/shard_map/all_to_all | solution.py:67
  568.8 22.5 %fusion.11 = (f32[192]{0:T(256)S(1)}, f32[192]{0:T(256)S(1)}, f32[192]{0:T(256)S(1)}, f32[192]{0:T(256)S(1)}, f32[192]{0:T(256)S(1)}, /*index=5*/f32[192]{0:T(256)S(1)}, f32[192,12288]{1,0:T(8,128)}) fusion(f32[192,12288]{1,0:T(8,128)} %get-tuple-element.33, f32[192]{0:T(256)S(1)} %get-tuple-element.10, s32[192]{0:T(256)S(1)} %get-tuple-element.17, ...), kind=kOutput, calls=%fused_computation.31 | convolution fusion | flops 646445952 | bytes 59826688 | tf_op jit(solution)/shard_map/dot_general | solution.py:71
  591.4 7.7 %fusion.65 = bf16[192,768]{1,0:T(8,128)(2,1)S(1)} fusion(bf16[12288,256]{1,0:T(8,128)(2,1)} %bitcast.7, f32[192,12288]{1,0:T(8,128)} %copy-done.1, f32[192]{0:T(256)S(1)} %get-tuple-element.11, f32[192]{0:T(256)S(1)} %get-tuple-element.9, s32[192]{0:T(256)S(1)} %get-tuple-element.17, s32[192]{0:T(256)S(1)} %get-tuple-element.16), kind=kOutput, calls=%fused_computation.77 | convolution fusion | flops 618184704 | bytes 12635136 | tf_op jit(solution)/shard_map/dot_general | solution.py:77
  601.3 12.1 %fusion.9 = (f32[192]{0:T(256)S(1)}, f32[192]{0:T(256)S(1)}, f32[192]{0:T(256)S(1)}, f32[192]{0:T(256)S(1)}) fusion(f32[192,12288]{1,0:T(8,128)S(1)} %bitcast.25, f32[192]{0:T(256)S(1)} %get-tuple-element.8, s32[192]{0:T(256)S(1)} %get-tuple-element.17, s32[192]{0:T(256)S(1)} %get-tuple-element.16, f32[192,12288]{1,0:T(8,128)} %get-tuple-element.34, ...), kind=kLoop, calls=%fused_computation.29 | loop fusion | flops 35388672 | bytes 37756416 | tf_op jit(solution)/shard_map/reduce_sum | solution.py:76
  613.4 7.6 %fusion.80 = bf16[192,768]{1,0:T(8,128)(2,1)S(1)} fusion(bf16[192,768]{1,0:T(8,128)(2,1)S(1)} %fusion.65, bf16[12288,256]{1,0:T(8,128)(2,1)} %bitcast.8, f32[192,12288]{1,0:T(8,128)} %get-tuple-element.34, f32[192]{0:T(256)S(1)} %get-tuple-element.5, f32[192]{0:T(256)S(1)} %get-tuple-element.13, s32[192]{0:T(256)S(1)} %get-tuple-element.17, ...), kind=kOutput, calls=%fused_computation.80 | convolution fusion | flops 618184704 | bytes 12636160 | tf_op jit(solution)/shard_map/dot_general | solution.py:77
  621.0 7.7 %fusion.95 = bf16[192,768]{1,0:T(8,128)(2,1)S(1)} fusion(bf16[192,768]{1,0:T(8,128)(2,1)S(1)} %fusion.80, bf16[12288,256]{1,0:T(8,128)(2,1)} %bitcast.9, f32[192,12288]{1,0:T(8,128)} %convolution_multiply_fusion.3, f32[192]{0:T(256)S(1)} %get-tuple-element.6, f32[192]{0:T(256)S(1)} %get-tuple-element.14, s32[192]{0:T(256)S(1)} %get-tuple-element.17, ...), kind=kOutput, calls=%fused_computation.83 | convolution fusion | flops 618184704 | bytes 12636160 | tf_op jit(solution)/shard_map/dot_general | solution.py:77
  638.7 7.7 %fusion.140 = bf16[192,768]{1,0:T(8,128)(2,1)S(1)} fusion(bf16[192,768]{1,0:T(8,128)(2,1)S(1)} %fusion.125, bf16[12288,256]{1,0:T(8,128)(2,1)} %bitcast.12, f32[192,12288]{1,0:T(8,128)} %get-tuple-element.33, f32[192]{0:T(256)S(1)} %get-tuple-element.10, f32[192]{0:T(256)S(1)} %get-tuple-element.4, s32[192]{0:T(256)S(1)} %get-tuple-element.17, ...), kind=kOutput, calls=%fused_computation.92 | convolution fusion | flops 618184704 | bytes 12636160 | tf_op jit(solution)/shard_map/dot_general | solution.py:77
  647.9 19.1 %reduce-scatter.2.cloned.1.call-done = bf16[192,768]{1,0:T(8,128)(2,1)} async-done(((bf16[192,1536]{1,0:T(8,128)(2,1)}), bf16[192,768]{1,0:T(8,128)(2,1)}) %reduce-scatter.2.cloned.1.call-update) | async-done | bytes 294928 | tf_op jit(solution)/shard_map/reduce_scatter | solution.py:83
  (77 shorter events, 58.8 us)
Async XLA Ops:
  7.2 639.2 %copy-start = (bf16[768,1536]{1,0:T(8,128)(2,1)S(1)}, bf16[768,1536]{1,0:T(8,128)(2,1)}, u32[]{:S(2)}) copy-start(bf16[768,1536]{1,0:T(8,128)(2,1)} %param.17) | copy-start | bytes 7077892
  11.7 15.2 %copy-start.6 = (f32[192]{0:T(256)}, f32[192]{0:T(256)S(1)}, u32[]{:S(2)}) copy-start(f32[192]{0:T(256)S(1)} %broadcast_multiply_fusion) | copy-start | bytes 2308
  12.0 14.9 %copy-start.8 = (f32[192]{0:T(256)}, f32[192]{0:T(256)S(1)}, u32[]{:S(2)}) copy-start(f32[192]{0:T(256)S(1)} %add_rsqrt_fusion) | copy-start | bytes 2308
  12.1 12.4 %copy-start.3 = (f32[3,1536]{1,0:T(4,128)S(1)}, f32[3,1536]{1,0:T(4,128)}, u32[]{:S(2)}) copy-start(f32[3,1536]{1,0:T(4,128)} %param.13) | copy-start | bytes 55300
  18.1 8.9 %copy-start.10 = (bf16[1536,768]{1,0:T(8,128)(2,1)S(1)}, bf16[1536,768]{1,0:T(8,128)(2,1)}, u32[]{:S(2)}) copy-start(bf16[1536,768]{1,0:T(8,128)(2,1)} %param.16) | copy-start | bytes 7077892
  31.3 90.7 %all-to-all-start = ((bf16[64,192,256]{2,1,0:T(8,128)(2,1)}), bf16[64,192,256]{2,1,0:T(8,128)(2,1)}, u32[]{:S(2)}, u32[]{:S(2)}) async-start(bf16[64,192,256]{2,1,0:T(8,128)(2,1)} %stack.12), calls=%async_computation | async-start | bytes 12582912 | tf_op jit(solution)/shard_map/all_to_all | solution.py:67
  125.4 88.3 %all-to-all-start.2 = ((bf16[64,192,256]{2,1,0:T(8,128)(2,1)}), bf16[64,192,256]{2,1,0:T(8,128)(2,1)}, u32[]{:S(2)}, u32[]{:S(2)}) async-start(bf16[64,192,256]{2,1,0:T(8,128)(2,1)} %stack.14), calls=%async_computation.2 | async-start | bytes 12582912 | tf_op jit(solution)/shard_map/all_to_all | solution.py:67
  217.1 83.9 %all-to-all-start.3 = ((bf16[64,192,256]{2,1,0:T(8,128)(2,1)}), bf16[64,192,256]{2,1,0:T(8,128)(2,1)}, u32[]{:S(2)}, u32[]{:S(2)}) async-start(bf16[64,192,256]{2,1,0:T(8,128)(2,1)} %stack.15), calls=%async_computation.3 | async-start | bytes 12582912 | tf_op jit(solution)/shard_map/all_to_all | solution.py:67
  304.4 86.3 %all-to-all-start.5 = ((bf16[64,192,256]{2,1,0:T(8,128)(2,1)}), bf16[64,192,256]{2,1,0:T(8,128)(2,1)}, u32[]{:S(2)}, u32[]{:S(2)}) async-start(bf16[64,192,256]{2,1,0:T(8,128)(2,1)} %stack.17), calls=%async_computation.5 | async-start | bytes 12582912 | tf_op jit(solution)/shard_map/all_to_all | solution.py:67
  394.1 85.7 %all-to-all-start.4 = ((bf16[64,192,256]{2,1,0:T(8,128)(2,1)}), bf16[64,192,256]{2,1,0:T(8,128)(2,1)}, u32[]{:S(2)}, u32[]{:S(2)}) async-start(bf16[64,192,256]{2,1,0:T(8,128)(2,1)} %stack.16), calls=%async_computation.4 | async-start | bytes 12582912 | tf_op jit(solution)/shard_map/all_to_all | solution.py:67
  483.3 13.6 %copy-start.11 = (s32[5]{0:T(128)S(1)}, s32[5]{0:T(128)}, u32[]{:S(2)}) copy-start(s32[5]{0:T(128)} %param.10) | copy-start | bytes 64
  483.3 13.8 %copy-start.5 = (f32[1536]{0:T(1024)S(1)}, f32[1536]{0:T(1024)}, u32[]{:S(2)}) copy-start(f32[1536]{0:T(1024)} %copy-done.4) | copy-start | bytes 18436
  483.3 13.8 %copy-start.7 = (f32[192]{0:T(256)S(1)}, f32[192]{0:T(256)}, u32[]{:S(2)}) copy-start(f32[192]{0:T(256)} %copy-done.6) | copy-start | bytes 2308
  483.3 13.9 %copy-start.9 = (f32[192]{0:T(256)S(1)}, f32[192]{0:T(256)}, u32[]{:S(2)}) copy-start(f32[192]{0:T(256)} %copy-done.8) | copy-start | bytes 2308
  483.3 85.5 %all-to-all-start.1 = ((bf16[64,192,256]{2,1,0:T(8,128)(2,1)}), bf16[64,192,256]{2,1,0:T(8,128)(2,1)}, u32[]{:S(2)}, u32[]{:S(2)}) async-start(bf16[64,192,256]{2,1,0:T(8,128)(2,1)} %stack.13), calls=%async_computation.1 | async-start | bytes 12582912 | tf_op jit(solution)/shard_map/all_to_all | solution.py:67
  496.8 170.2 %reduce-scatter.2.cloned.1.call-start = ((), (), s32[]{:S(2)}) async-start(), calls=%async_computation.7 | async-start | bytes 884736 | tf_op jit(solution)/shard_map/reduce_scatter | solution.py:83
  523.7 3.5 copy-start.1
  591.3 7.8 %slice-start = ((s8[9437184]{0:T(1024)(128)(4,1)}), s8[4194304]{0:T(1024)(128)(4,1)S(1)}, s32[]{:S(2)}) async-start(s8[9437184]{0:T(1024)(128)(4,1)} %bitcast.24), calls=%async_computation.8 | async-start | bytes 8388608
  591.3 7.8 %slice-start.3 = ((s8[9437184]{0:T(1024)(128)(4,1)}), s8[4194304]{0:T(1024)(128)(4,1)S(1)}, s32[]{:S(2)}) async-start(s8[9437184]{0:T(1024)(128)(4,1)} %bitcast.26), calls=%async_computation.11 | async-start | bytes 8388608
  591.4 8.2 %slice-start.1 = ((s8[9437184]{0:T(1024)(128)(4,1)}), s8[4194304]{0:T(1024)(128)(4,1)S(1)}, s32[]{:S(2)}) async-start(s8[9437184]{0:T(1024)(128)(4,1)} %bitcast.24), calls=%async_computation.9 | async-start | bytes 8388608
  591.4 8.4 %slice-start.2 = ((s8[9437184]{0:T(1024)(128)(4,1)}), s8[1048576]{0:T(1024)(128)(4,1)S(1)}, s32[]{:S(2)}) async-start(s8[9437184]{0:T(1024)(128)(4,1)} %bitcast.24), calls=%async_computation.10 | async-start | bytes 2097152
  591.4 9.7 %slice-start.4 = ((s8[9437184]{0:T(1024)(128)(4,1)}), s8[4194304]{0:T(1024)(128)(4,1)S(1)}, s32[]{:S(2)}) async-start(s8[9437184]{0:T(1024)(128)(4,1)} %bitcast.26), calls=%async_computation.12 | async-start | bytes 8388608
  591.4 9.9 %slice-start.5 = ((s8[9437184]{0:T(1024)(128)(4,1)}), s8[1048576]{0:T(1024)(128)(4,1)S(1)}, s32[]{:S(2)}) async-start(s8[9437184]{0:T(1024)(128)(4,1)} %bitcast.26), calls=%async_computation.13 | async-start | bytes 2097152
  638.7 28.3 %copy-start.2 = (bf16[192,768]{1,0:T(8,128)(2,1)S(1)}, bf16[192,768]{1,0:T(8,128)(2,1)}, u32[]{:S(2)}) copy-start(bf16[192,768]{1,0:T(8,128)(2,1)} %param.9) | copy-start | bytes 884740
  (1 other events, 2.4 us)
Sparse Core Ops, SparseCore 0:
  648.0 19.0 reduce-scatter.1
